TPU v7x, 32 devices: a whole 2x2x4 slice. The times are simulated.
32 devices in a mesh: row: 4 (over y, x), col: 8 (over z, core).
Axes of the slice: x: 2, y: 2, z: 4, core: 2. Of those that a mesh axis runs over, the one named last changes fastest.
Arguments:
- throat_owner: int32 [16384, 1], P(('row', 'col')), may hold values from 0 to 3; in each aligned block of 512 rows (0 to 511, 512 to 1023, ...) at most 128 rows name the same one
- throat_interior: int32 [16384], P(('row', 'col')), may hold values from 0 to 895
- throat_offset: int32 [16384], P(('row', 'col')), may hold values from 0 to 4095
- throat_conductance: float32 [16384], P(('row', 'col')), may hold values from 0.1 to 1
- child_update: bfloat16 [7168, 16384], P('col', 'row'), may hold values from -0.09375 to 0.09375
- panel_pores: int32 [4096], replicated, may hold values from 0 to 16383, as said below
- interior_inverse: bfloat16 [7168, 896], P('col'), as said below
- separator_rows: float32 [4096, 16384], P('col', 'row'), may hold values from -6 to 6
Outputs:
- schur_rows: float32 [4096, 16384], P('col', 'row')
Inputs may be any that keep to these rules, and one draw needn't show every extreme that they name: `throat_owner`: in each device's block of 512 throats no owner is named more than 128 times, a bound that some block reaches. `panel_pores`: the 4096 pores are distinct; at most 1536 of them lie in any one owner's range of 4096 pores, and one owner holds exactly 1536. `interior_inverse`: each group's block of 896 rows is lower triangular with diagonal entries between 0.8 and 1.2.
All inputs are finite; a program needn't handle non-finite values.
Results may differ from a plain program's by a relative error of at most 0.01.
Values may be sent and summed in bfloat16 or wider, within the bound.
No kernel may reach another device: no remote copies, remote signals or barrier semaphores. Data moves between devices by JAX's collectives and lax.ppermute only.
A program may use at most 128 MiB of HBM per device.

v0:
```python
import jax
import jax.numpy as jnp
from jax import lax
from jax.sharding import PartitionSpec as P


def rank_within(owners, owner_count):
    onehot = (owners[:, None] == jnp.arange(owner_count, dtype=jnp.int32)[None, :]).astype(
        jnp.int32
    )
    before = jnp.cumsum(onehot, axis=0) - onehot
    return jnp.sum(before * onehot, axis=1)


def panel_slots(panel_pores, owner_width, row_count, row_index):
    panel_total = panel_pores.shape[0]
    panel_owner = panel_pores // owner_width
    panel_within = rank_within(panel_owner, row_count)
    panel_limit = 3 * panel_total // (2 * row_count)
    picked = jnp.where(panel_owner == row_index, panel_within, panel_limit)
    chosen = (
        jnp.zeros((panel_limit,), jnp.int32)
        .at[picked]
        .set(panel_pores - panel_owner * owner_width, mode="drop")
    )
    placed = panel_owner * panel_limit + panel_within
    return (chosen, placed)


def per_device(
    throat_owner,
    throat_interior,
    throat_offset,
    throat_conductance,
    child_update,
    panel_pores,
    interior_inverse,
    separator_rows,
):
    row_count = lax.axis_size("row")
    row_index = lax.axis_index("row")
    owner_width = separator_rows.shape[1]
    throats = throat_interior.shape[0]
    slot_limit = throats // 4
    owners = throat_owner[:, 0]
    slot_ids = owners * slot_limit + rank_within(owners, row_count)
    total_slots = row_count * slot_limit
    rows_sent = jnp.zeros((total_slots,), jnp.int32).at[slot_ids].set(throat_interior)
    cols_sent = jnp.zeros((total_slots,), jnp.int32).at[slot_ids].set(throat_offset)
    values_sent = jnp.zeros((total_slots,), jnp.float32).at[slot_ids].set(throat_conductance)
    index_block = jnp.stack(
        [rows_sent.reshape(row_count, slot_limit), cols_sent.reshape(row_count, slot_limit)], axis=1
    )
    index_back, values_back = (
        lax.all_to_all(index_block, "row", split_axis=0, concat_axis=0, tiled=True),
        lax.all_to_all(
            values_sent.reshape(row_count, slot_limit),
            "row",
            split_axis=0,
            concat_axis=0,
            tiled=True,
        ),
    )
    summed = (
        child_update.astype(jnp.float32)
        .at[index_back[:, 0, :].ravel(), index_back[:, 1, :].ravel()]
        .add(values_back.ravel())
    )
    coupling = summed.astype(jnp.bfloat16)
    solved = jnp.dot(interior_inverse, coupling, preferred_element_type=jnp.float32).astype(
        jnp.bfloat16
    )
    chosen, placed = panel_slots(panel_pores, owner_width, row_count, row_index)
    local_columns = jnp.take(solved, chosen, axis=1)
    gathered = lax.all_gather(local_columns, "row", axis=1, tiled=True)
    panel_solved = jnp.take(gathered, placed, axis=1)
    update = lax.psum_scatter(
        jnp.dot(panel_solved.T, solved, preferred_element_type=jnp.float32).astype(jnp.bfloat16),
        "col",
        scatter_dimension=0,
        tiled=True,
    ).astype(jnp.float32)
    return separator_rows - update


def solution(mesh):
    in_specs = (
        P(("row", "col"), None),
        P(("row", "col")),
        P(("row", "col")),
        P(("row", "col")),
        P("col", "row"),
        P(),
        P("col", None),
        P("col", "row"),
    )
    out_specs = P("col", "row")
    return jax.shard_map(
        per_device, mesh=mesh, in_specs=in_specs, out_specs=out_specs, check_vma=False
    )
```

profile of v0, /device:TPU:0, one launch (start us, length us, event | category | flops | bytes accessed | tf_op | source)
XLA Modules:
  0.0 674.5 jit_solution(6133341720263990972)
XLA Ops:
  6.5 0.0 copy-start
  6.5 0.8 fusion.17
  7.3 1.2 reduce-window.16
  8.6 0.2 slice_reduce_fusion.1
  8.8 0.2 reduce-window.19
  8.9 0.1 add_bitcast_fusion.1
  9.0 0.7 fusion.16
  9.7 0.7 compare_select_fusion.5
  10.4 2.6 scatter_custom_fusion.2
  13.0 2.6 scatter_custom_fusion.1
  15.6 0.6 pad_add_fusion
  16.2 5.2 all-to-all-start
  21.4 0.7 add_select_fusion
  22.1 1.2 reduce-window.14
  23.3 0.2 slice_reduce_fusion
  23.5 0.2 reduce-window.15
  23.7 0.1 add_bitcast_fusion
  23.8 0.1 fusion.10
  23.9 0.7 broadcast_clamp_fusion
  24.7 15.5 %scatter_custom_fusion = s32[1536]{0:T(1024)S(1)} fusion(s32[4096]{0:T(1024)S(1)} %get-tuple-element.6, s32[4096]{0:T(1024)S(1)} %get-tuple-element.7, s32[]{:T(128)} %constant.39.clone.1), kind=kCustom, calls=%fused_computation.54 | custom fusion | bytes 6148 | tf_op jit(solution)/shard_map/scatter | solution.py:24
  40.2 10.3 %convert_element_type.34 = f32[896,4096]{1,0:T(8,128)} convert(bf16[896,4096]{1,0:T(8,128)(2,1)} %param.12) | non-fusion elementwise | flops 3670016 | bytes 22020096 | tf_op jit(solution)/shard_map/convert_element_type | solution.py:65
  50.5 3.2 scatter_custom_fusion.3
  53.7 0.0 all-to-all-done
  53.7 4.2 all-to-all-start.1
  57.9 0.0 all-gather.2.cloned.1.call-start
  57.9 4.5 all-to-all-done.1
  62.4 61.5 %scatter_fusion = f32[896,4096]{1,0:T(8,128)} fusion(f32[896,4096]{1,0:T(8,128)} %convert_element_type.34, s32[512]{0:T(512)S(1)} %bitcast.67, f32[512]{0:T(512)S(1)} %bitcast.70), kind=kCustom, calls=%fused_computation.6 | custom fusion | flops 512 | bytes 10240 | tf_op jit(solution)/shard_map/scatter-add | solution.py:67
  123.8 0.0 copy-done
  123.8 16.1 %fusion.4 = bf16[4096,896]{1,0:T(8,128)(2,1)} fusion(bf16[896,896]{1,0:T(8,128)(2,1)S(1)} %copy-done, f32[896,4096]{1,0:T(8,128)} %scatter_fusion), kind=kOutput, calls=%fused_computation.13 | convolution fusion | flops 6584008704 | bytes 23625728 | tf_op jit(solution)/shard_map/dot_general | solution.py:70
  139.9 11.1 %gather_fusion = bf16[1536,896]{1,0:T(8,128)(2,1)} fusion(bf16[896,4096]{0,1:T(8,128)(2,1)} %bitcast.66, s32[2048]{0:T(1024)S(1)} %pad_clamp_fusion), kind=kCustom, calls=%fused_computation | custom fusion | bytes 5511168 | tf_op jit(solution)/shard_map/jit(_take)/gather | solution.py:74
  151.0 0.0 copy-start.2
  151.0 3.8 select_bitcast_fusion
  154.8 0.0 all-gather.2.cloned.1.call-update
  154.9 0.3 reduce-scatter.2.cloned.1.call-start
  155.1 0.0 copy-done.2
  155.2 108.6 %all-gather.2.cloned.1.call-done = bf16[896,6144]{0,1:T(8,128)(2,1)} async-done(((bf16[896,1536]{0,1:T(8,128)(2,1)}), bf16[896,6144]{0,1:T(8,128)(2,1)}) %all-gather.2.cloned.1.call-update) | async-done | bytes 11010064 | tf_op jit(solution)/shard_map/all_gather | solution.py:75
  263.8 25.3 %gather_fusion.1 = bf16[4096,896]{1,0:T(8,128)(2,1)} fusion(bf16[896,6144]{0,1:T(8,128)(2,1)} %all-gather.2.cloned.1.call-done, s32[4096]{0:T(1024)S(1)} %get-tuple-element.5), kind=kCustom, calls=%fused_computation.1 | custom fusion | bytes 14696448 | tf_op jit(solution)/shard_map/jit(_take)/gather | solution.py:76
  289.1 43.1 %convolution_convert_fusion = bf16[4096,4096]{1,0:T(8,128)(2,1)} fusion(bf16[4096,896]{1,0:T(8,128)(2,1)} %fusion.4, bf16[4096,896]{1,0:T(8,128)(2,1)} %gather_fusion.1, pred[4096]{0:T(1024)(128)(4,1)S(1)} %compare_and_fusion), kind=kOutput, calls=%fused_computation.7 | convolution fusion | flops 30085218304 | bytes 48238592 | tf_op jit(solution)/shard_map/dot_general | solution.py:78
  332.2 0.0 reduce-scatter.2.cloned.1.call-update
  332.2 0.0 copy-start.1
  332.2 325.7 %reduce-scatter.2.cloned.1.call-done = bf16[512,4096]{1,0:T(8,128)(2,1)} async-done(((bf16[4096,4096]{1,0:T(8,128)(2,1)}), bf16[512,4096]{1,0:T(8,128)(2,1)}) %reduce-scatter.2.cloned.1.call-update) | async-done | bytes 4194320 | tf_op jit(solution)/shard_map/reduce_scatter | solution.py:77
  657.9 9.7 %convert_subtract_fusion = f32[512,4096]{1,0:T(8,128)} fusion(f32[512,4096]{1,0:T(8,128)} %param.15, bf16[512,4096]{1,0:T(8,128)(2,1)} %reduce-scatter.2.cloned.1.call-done), kind=kLoop, calls=%fused_computation.8 | loop fusion | flops 4194304 | bytes 20971520 | tf_op jit(solution)/shard_map/sub | solution.py:83
  667.6 0.0 copy-done.1
  (6 shorter events, 0.1 us)
Async XLA Ops:
  6.5 117.3 %copy-start = (bf16[896,896]{1,0:T(8,128)(2,1)S(1)}, bf16[896,896]{1,0:T(8,128)(2,1)}, u32[]{:S(2)}) copy-start(bf16[896,896]{1,0:T(8,128)(2,1)} %param.14) | copy-start | bytes 4816900
  16.2 37.5 %all-to-all-start = ((s32[4,2,128]{2,1,0:T(2,128)}), s32[4,2,128]{2,1,0:T(2,128)S(1)}, u32[]{:S(2)}, u32[]{:S(2)}) async-start(s32[4,2,128]{2,1,0:T(2,128)} %pad_add_fusion), calls=%async_computation | async-start | bytes 8192 | tf_op jit(solution)/shard_map/all_to_all | solution.py:55
  53.7 8.7 %all-to-all-start.1 = ((f32[4,1,128]{2,1,0:T(1,128)}), f32[4,1,128]{2,1,0:T(1,128)S(1)}, u32[]{:S(2)}, u32[]{:S(2)}) async-start(f32[4,1,128]{2,1,0:T(1,128)} %bitcast.12), calls=%async_computation.1 | async-start | bytes 4096 | tf_op jit(solution)/shard_map/all_to_all | solution.py:56
  57.9 205.9 %all-gather.2.cloned.1.call-start = ((), (), s32[]{:S(2)}) async-start(), calls=%async_computation.3 | async-start | bytes 13762560 | tf_op jit(solution)/shard_map/all_gather | solution.py:75
  151.0 4.1 copy-start.2
  154.9 503.1 %reduce-scatter.2.cloned.1.call-start = ((), (), s32[]{:S(2)}) async-start(), calls=%async_computation.4 | async-start | bytes 37748736 | tf_op jit(solution)/shard_map/reduce_scatter | solution.py:77
  332.2 335.4 %copy-start.1 = (bf16[896,896]{1,0:T(8,128)(2,1)S(1)}, bf16[896,896]{1,0:T(8,128)(2,1)}, u32[]{:S(2)}) copy-start(bf16[896,896]{1,0:T(8,128)(2,1)} %param.14) | copy-start | bytes 4816900
Sparse Core Ops, SparseCore 0:
  155.0 108.7 all-gather.1
  332.4 325.5 reduce-scatter.1
where the time goes:
time: 676 us; the launch traced here: 674 us
  waiting for transfers between devices  439 us (65%)
  other arithmetic  92.6 us (14%)
  local copies, waits for them, and re-layouts  60.7 us (9%)
  matrix products  59.1 us (9%)
  between operations  13.5 us (2%)
  starting transfers between devices  9.62 us (1%)
    reduce_scatter x1, waiting for transfers between devices, per_device(): lax.psum_scatter(jnp.dot(panel_solved.T, solved, preferred_element_type=j...  326 us
    all_gather x1, waiting for transfers between devices, per_device(): gathered = lax.all_gather(local_columns, 'row', axis=1, tiled=True)  109 us
    scatter-add x1, other arithmetic, per_device(): summed = child_update.astype(jnp.float32).at[index_back[:, 0, :].ravel(),...  61.5 us
    dot_general x1, matrix products, per_device(): jnp.dot(panel_solved.T, solved, preferred_element_type=jnp.float32)  43.1 us
    gather x1, local copies, waits for them, and re-layouts, per_device(): panel_solved = jnp.take(gathered, placed, axis=1)  25.3 us
    dot_general x1, matrix products, per_device(): jnp.dot(interior_inverse, coupling, preferred_element_type=jnp.float32)  16.1 us
    scatter x1, local copies, waits for them, and re-layouts, panel_slots(): chosen = jnp.zeros((panel_limit,), jnp.int32).at[picked].set(panel_pores...  15.5 us
  transfers between devices with their start and end apart: 4, of which 3 were waited for; matrix products, arithmetic and copies ran while one was open for 5% of the time, Pallas kernels for 0%

commit v1 on v0

--- a/solution.py
+++ b/solution.py
@@ -2,6 +2,23 @@
 import jax.numpy as jnp
 from jax import lax
 from jax.sharding import PartitionSpec as P
+
+
+def joined_along(pieces, dim):
+    shape = list(pieces.shape[1:])
+    shape[dim] *= pieces.shape[0]
+    return jnp.moveaxis(pieces, 0, dim).reshape(shape)
+
+
+def grow_blocks(x, axis):
+    devices, index = (lax.axis_size(axis), lax.axis_index(axis))
+    parts, bit = (x[None], 1)
+    while bit < devices:
+        other = lax.ppermute(parts, axis, [(i, i ^ bit) for i in range(devices)])
+        low = index & bit == 0
+        parts = jnp.concatenate([jnp.where(low, parts, other), jnp.where(low, other, parts)])
+        bit *= 2
+    return parts
 
 
 def rank_within(owners, owner_count):
@@ -72,7 +89,7 @@
     )
     chosen, placed = panel_slots(panel_pores, owner_width, row_count, row_index)
     local_columns = jnp.take(solved, chosen, axis=1)
-    gathered = lax.all_gather(local_columns, "row", axis=1, tiled=True)
+    gathered = joined_along(grow_blocks(local_columns, "row"), 1)
     panel_solved = jnp.take(gathered, placed, axis=1)
     update = lax.psum_scatter(
         jnp.dot(panel_solved.T, solved, preferred_element_type=jnp.float32).astype(jnp.bfloat16),

time: 676 us -> 762 us (1.13)
  waiting for transfers between devices: 439 us -> 507 us
  other arithmetic: 92.6 us -> 109 us
    ppermute x0 -> x2, waiting for transfers between devices: none -> 177 us  [grow_blocks(): other = lax.ppermute(parts, axis, [(i, i ^ bit) for i in range(devices)])]
    all_gather x1 -> x0, waiting for transfers between devices: 109 us -> none  [per_device(): gathered = lax.all_gather(local_columns, 'row', axis=1, tiled=True)]
    concatenate x0 -> x2, other arithmetic: none -> 8.29 us  [grow_blocks(): jnp.concatenate([jnp.where(low, parts, other), jnp.where(low, other, part...]
    select_n x0 -> x2, other arithmetic: none -> 8.13 us  [grow_blocks(): jnp.where(low, parts, other)]
  transfers between devices with their start and end apart: 4 -> 5, of which waited for: 3 -> 4; matrix products, arithmetic and copies ran while one was open for 5% -> 4% of each run, Pallas kernels for 0% -> 0%
where the time goes in v1:
time: 762 us; the launch traced here: 760 us
  waiting for transfers between devices  507 us (67%)
  other arithmetic  109 us (14%)
  local copies, waits for them, and re-layouts  61.7 us (8%)
  matrix products  59.1 us (8%)
  between operations  13.5 us (2%)
  starting transfers between devices  10.3 us (1%)
    reduce_scatter x1, waiting for transfers between devices, per_device(): lax.psum_scatter(jnp.dot(panel_solved.T, solved, preferred_element_type=j...  325 us
    ppermute x2, waiting for transfers between devices, grow_blocks(): other = lax.ppermute(parts, axis, [(i, i ^ bit) for i in range(devices)])  177 us
    scatter-add x1, other arithmetic, per_device(): summed = child_update.astype(jnp.float32).at[index_back[:, 0, :].ravel(),...  61.5 us
    dot_general x1, matrix products, per_device(): jnp.dot(panel_solved.T, solved, preferred_element_type=jnp.float32)  43.1 us
    gather x1, local copies, waits for them, and re-layouts, per_device(): panel_solved = jnp.take(gathered, placed, axis=1)  25.5 us
    dot_general x1, matrix products, per_device(): jnp.dot(interior_inverse, coupling, preferred_element_type=jnp.float32)  16.1 us
    scatter x1, local copies, waits for them, and re-layouts, panel_slots(): chosen = jnp.zeros((panel_limit,), jnp.int32).at[picked].set(panel_pores...  15.5 us
  transfers between devices with their start and end apart: 5, of which 4 were waited for; matrix products, arithmetic and copies ran while one was open for 4% of the time, Pallas kernels for 0%

profile of v1, /device:TPU:0, one launch (start us, length us, event | category | flops | bytes accessed | tf_op | source)
XLA Modules:
  0.0 760.2 jit_solution(14939404080508389294)
XLA Ops:
  6.5 0.0 copy-start
  6.5 0.8 fusion.17
  7.3 1.2 reduce-window.16
  8.6 0.2 slice_reduce_fusion.1
  8.8 0.2 reduce-window.19
  8.9 0.1 add_bitcast_fusion.1
  9.0 0.7 fusion.16
  9.7 0.7 compare_select_fusion.5
  10.4 2.6 scatter_custom_fusion.2
  13.0 2.6 scatter_custom_fusion.1
  15.6 0.6 pad_add_fusion
  16.2 5.2 all-to-all-start
  21.4 0.7 add_select_fusion
  22.1 1.2 reduce-window.14
  23.3 0.2 slice_reduce_fusion
  23.5 0.2 reduce-window.15
  23.7 0.1 add_bitcast_fusion
  23.8 0.1 fusion.10
  23.9 0.7 broadcast_clamp_fusion
  24.7 15.5 %scatter_custom_fusion = s32[1536]{0:T(1024)S(1)} fusion(s32[4096]{0:T(1024)S(1)} %get-tuple-element.10, s32[4096]{0:T(1024)S(1)} %get-tuple-element.11, s32[]{:T(128)} %constant.39.clone.1), kind=kCustom, calls=%fused_computation.60 | custom fusion | bytes 6148 | tf_op jit(solution)/shard_map/scatter | solution.py:41
  40.2 10.3 %convert_element_type.34 = f32[896,4096]{1,0:T(8,128)} convert(bf16[896,4096]{1,0:T(8,128)(2,1)} %param.12) | non-fusion elementwise | flops 3670016 | bytes 22020096 | tf_op jit(solution)/shard_map/convert_element_type | solution.py:82
  50.5 3.2 scatter_custom_fusion.3
  53.7 0.0 all-to-all-done
  53.7 4.2 all-to-all-start.1
  57.9 0.0 reduce-scatter.2.cloned.1.call-start
  57.9 4.5 all-to-all-done.1
  62.4 61.5 %scatter_fusion = f32[896,4096]{1,0:T(8,128)} fusion(f32[896,4096]{1,0:T(8,128)} %convert_element_type.34, s32[512]{0:T(512)S(1)} %bitcast.75, f32[512]{0:T(512)S(1)} %bitcast.78), kind=kCustom, calls=%fused_computation.6 | custom fusion | flops 512 | bytes 10240 | tf_op jit(solution)/shard_map/scatter-add | solution.py:84
  123.8 0.0 copy-done
  123.8 16.1 %fusion.4 = bf16[4096,896]{1,0:T(8,128)(2,1)} fusion(bf16[896,896]{1,0:T(8,128)(2,1)S(1)} %copy-done, f32[896,4096]{1,0:T(8,128)} %scatter_fusion), kind=kOutput, calls=%fused_computation.14 | convolution fusion | flops 6584008704 | bytes 23625728 | tf_op jit(solution)/shard_map/dot_general | solution.py:87
  139.9 11.1 %gather_fusion = bf16[1536,896]{1,0:T(8,128)(2,1)} fusion(bf16[896,4096]{0,1:T(8,128)(2,1)} %bitcast.74, s32[2048]{0:T(1024)S(1)} %pad_clamp_fusion), kind=kCustom, calls=%fused_computation | custom fusion | bytes 5511168 | tf_op jit(solution)/shard_map/jit(_take)/gather | solution.py:91
  151.0 3.7 bitcast_select_fusion
  154.7 0.6 collective-permute-start
  155.3 59.4 %collective-permute-done = bf16[1,896,1536]{1,2,0:T(8,128)(2,1)} collective-permute-done((bf16[1,896,1536]{1,2,0:T(8,128)(2,1)}, bf16[1,896,1536]{1,2,0:T(8,128)(2,1)}, u32[]{:S(2)}, u32[]{:S(2)}) %collective-permute-start) | collective-permute-done | bytes 2752544 | tf_op jit(solution)/shard_map/ppermute | solution.py:17
  214.7 3.2 broadcast_select_fusion.3
  217.8 0.0 copy-start.2
  217.9 0.0 copy-start.4
  217.9 3.3 pad_maximum_fusion.1
  221.2 0.8 copy-done.3
  222.0 0.3 collective-permute-start.1
  222.3 117.7 %collective-permute-done.1 = bf16[2,896,1536]{1,2,0:T(8,128)(2,1)} collective-permute-done((bf16[2,896,1536]{1,2,0:T(8,128)(2,1)}, bf16[2,896,1536]{1,2,0:T(8,128)(2,1)}, u32[]{:S(2)}, u32[]{:S(2)}) %collective-permute-start.1) | collective-permute-done | bytes 5505056 | tf_op jit(solution)/shard_map/ppermute | solution.py:17
  340.0 5.0 broadcast_select_fusion.1
  345.0 5.0 pad_maximum_fusion
  350.0 25.5 %gather_fusion.1 = bf16[4096,896]{1,0:T(8,128)(2,1)} fusion(bf16[896,6144]{0,1:T(8,128)(2,1)} %bitcast.73, s32[4096]{0:T(1024)S(1)} %get-tuple-element.9), kind=kCustom, calls=%fused_computation.1 | custom fusion | bytes 14696448 | tf_op jit(solution)/shard_map/jit(_take)/gather | solution.py:93
  375.5 43.1 %convolution_convert_fusion = bf16[4096,4096]{1,0:T(8,128)(2,1)} fusion(bf16[4096,896]{1,0:T(8,128)(2,1)} %fusion.4, bf16[4096,896]{1,0:T(8,128)(2,1)} %gather_fusion.1, pred[4096]{0:T(1024)(128)(4,1)S(1)} %compare_and_fusion), kind=kOutput, calls=%fused_computation.7 | convolution fusion | flops 30085218304 | bytes 48238592 | tf_op jit(solution)/shard_map/dot_general | solution.py:95
  418.6 0.0 reduce-scatter.2.cloned.1.call-update
  418.6 0.0 copy-start.1
  418.6 325.0 %reduce-scatter.2.cloned.1.call-done = bf16[512,4096]{1,0:T(8,128)(2,1)} async-done(((bf16[4096,4096]{1,0:T(8,128)(2,1)}), bf16[512,4096]{1,0:T(8,128)(2,1)}) %reduce-scatter.2.cloned.1.call-update) | async-done | bytes 4194320 | tf_op jit(solution)/shard_map/reduce_scatter | solution.py:94
  743.6 9.7 %convert_subtract_fusion = f32[512,4096]{1,0:T(8,128)} fusion(f32[512,4096]{1,0:T(8,128)} %param.15, bf16[512,4096]{1,0:T(8,128)(2,1)} %reduce-scatter.2.cloned.1.call-done), kind=kLoop, calls=%fused_computation.9 | loop fusion | flops 4194304 | bytes 20971520 | tf_op jit(solution)/shard_map/sub | solution.py:100
  (10 shorter events, 0.1 us)
Async XLA Ops:
  6.5 117.3 %copy-start = (bf16[896,896]{1,0:T(8,128)(2,1)S(1)}, bf16[896,896]{1,0:T(8,128)(2,1)}, u32[]{:S(2)}) copy-start(bf16[896,896]{1,0:T(8,128)(2,1)} %param.14) | copy-start | bytes 4816900
  16.2 37.5 %all-to-all-start = ((s32[4,2,128]{2,1,0:T(2,128)}), s32[4,2,128]{2,1,0:T(2,128)S(1)}, u32[]{:S(2)}, u32[]{:S(2)}) async-start(s32[4,2,128]{2,1,0:T(2,128)} %pad_add_fusion), calls=%async_computation | async-start | bytes 8192 | tf_op jit(solution)/shard_map/all_to_all | solution.py:72
  53.7 8.7 %all-to-all-start.1 = ((f32[4,1,128]{2,1,0:T(1,128)}), f32[4,1,128]{2,1,0:T(1,128)S(1)}, u32[]{:S(2)}, u32[]{:S(2)}) async-start(f32[4,1,128]{2,1,0:T(1,128)} %bitcast.12), calls=%async_computation.1 | async-start | bytes 4096 | tf_op jit(solution)/shard_map/all_to_all | solution.py:73
  57.9 685.8 %reduce-scatter.2.cloned.1.call-start = ((), (), s32[]{:S(2)}) async-start(), calls=%async_computation.3 | async-start | bytes 37748736 | tf_op jit(solution)/shard_map/reduce_scatter | solution.py:94
  154.7 60.0 %collective-permute-start = (bf16[1,896,1536]{1,2,0:T(8,128)(2,1)}, bf16[1,896,1536]{1,2,0:T(8,128)(2,1)}, u32[]{:S(2)}, u32[]{:S(2)}) collective-permute-start(bf16[1,896,1536]{1,2,0:T(8,128)(2,1)} %bitcast_select_fusion), channel_id=1, source_target_pairs={{0,8},{8,0},{16,24},{24,16},{1,9},{9,1},{17,25},{25,17},{2,10},{10... | collective-permute-start | bytes 8257544 | tf_op jit(solution)/shard_map/ppermute | solution.py:17
  217.8 3.4 copy-start.2
  217.9 4.1 copy-start.3
  217.9 4.5 copy-start.4
  222.0 118.0 %collective-permute-start.1 = (bf16[2,896,1536]{1,2,0:T(8,128)(2,1)}, bf16[2,896,1536]{1,2,0:T(8,128)(2,1)}, u32[]{:S(2)}, u32[]{:S(2)}) collective-permute-start(bf16[2,896,1536]{1,2,0:T(8,128)(2,1)} %pad_maximum_fusion.1), channel_id=1, source_target_pairs={{0,16},{8,24},{16,0},{24,8},{1,17},{9,25},{17,1},{25,9},{2,18},{10... | collective-permute-start | bytes 16515080 | tf_op jit(solution)/shard_map/ppermute | solution.py:17
  418.6 334.7 %copy-start.1 = (bf16[896,896]{1,0:T(8,128)(2,1)S(1)}, bf16[896,896]{1,0:T(8,128)(2,1)}, u32[]{:S(2)}) copy-start(bf16[896,896]{1,0:T(8,128)(2,1)} %param.14) | copy-start | bytes 4816900
Sparse Core Ops, SparseCore 0:
  418.7 324.8 reduce-scatter.1
